TPU v7x, 32 devices: a whole 2x2x4 slice. The times are simulated.
32 devices in a mesh: dp: 16 (over z, y, core), tensor: 2 (over x).
Axes of the slice: x: 2, y: 2, z: 4, core: 2. Of those that a mesh axis runs over, the one named last changes fastest.
Arguments:
- tokens: bfloat16 [16384, 768], P(('dp', 'tensor')), may hold values from -6 to 6
- query_weight: bfloat16 [768, 768], P('dp', 'tensor'), may hold values from -0.21875 to 0.21875
- query_bias: float32 [768], replicated, may hold values from -3 to 3
- key_weight: bfloat16 [768, 768], P('dp', 'tensor'), may hold values from -0.21875 to 0.21875
- value_weight: bfloat16 [768, 768], P('dp', 'tensor'), may hold values from -0.21875 to 0.21875
- value_bias: float32 [768], replicated, may hold values from -0.625 to 0.625
- output_weight: bfloat16 [768, 768], P('tensor', 'dp'), may hold values from -1.25 to 1.25
- output_bias: float32 [768], replicated, may hold values from -3 to 3
- first_gain: float32 [768], replicated, may hold values from 0.5 to 1.5
- first_shift: float32 [768], replicated, may hold values from -3 to 3
- inner_weight: bfloat16 [768, 3072], P('dp', 'tensor'), may hold values from -0.21875 to 0.21875
- inner_bias: float32 [3072], replicated, may hold values from -3 to 3
- outer_weight: bfloat16 [3072, 768], P('tensor', 'dp'), may hold values from -0.109375 to 0.109375
- outer_bias: float32 [768], replicated, may hold values from -3 to 3
- second_gain: float32 [768], replicated, may hold values from 0.5 to 1.5
- second_shift: float32 [768], replicated, may hold values from -3 to 3
- segments: int32 [16, 1024], P('dp'), may hold values from 0 to 7, never falling along the last dimension, each value on 1 to 768 neighbouring positions
- valid_length: int32 [16], P('dp'), may hold values from 512 to 1024
- cotangent: bfloat16 [16384, 768], P(('dp', 'tensor')), may hold values from -6 to 6
Outputs:
- layer_output: bfloat16 [16384, 768], P(('dp', 'tensor'))
- input_gradient: float32 [16384, 768], P(('dp', 'tensor'))
- query_weight_gradient: float32 [768, 768], P('dp', 'tensor')
- query_bias_gradient: float32 [768], replicated
- key_weight_gradient: float32 [768, 768], P('dp', 'tensor')
- value_weight_gradient: float32 [768, 768], P('dp', 'tensor')
- value_bias_gradient: float32 [768], replicated
- output_weight_gradient: float32 [768, 768], P('tensor', 'dp')
- output_bias_gradient: float32 [768], replicated
- first_gain_gradient: float32 [768], replicated
- first_shift_gradient: float32 [768], replicated
- inner_weight_gradient: float32 [768, 3072], P('dp', 'tensor')
- inner_bias_gradient: float32 [3072], replicated
- outer_weight_gradient: float32 [3072, 768], P('tensor', 'dp')
- outer_bias_gradient: float32 [768], replicated
- second_gain_gradient: float32 [768], replicated
- second_shift_gradient: float32 [768], replicated
Inputs may be any that keep to these rules, and one draw needn't show every extreme that they name: `segments`: segment numbers never fall along a sequence; a token attends only to tokens of its own document. tokens of a sequence at positions valid_length and beyond are padding: no query attends to them as keys except the token itself.
All inputs are finite; a program needn't handle non-finite values.
Results may differ from a plain program's by a relative error of at most 0.013.
Values may be sent and summed in bfloat16 or wider, within the bound.
No kernel may reach another device: no remote copies, remote signals or barrier semaphores. Data moves between devices by JAX's collectives and lax.ppermute only.
A program may use at most 128 MiB of HBM per device.

v0:
```python
import jax
import jax.numpy as jnp
from jax import lax
from jax.sharding import PartitionSpec as P

HEAD_DIM = 64


norm_epsilon = 1e-12
masked_score = -1e30


def normalize(matrix, gain, shift):
    center = matrix - jnp.mean(matrix, axis=-1, keepdims=True)
    spread = jnp.mean(center * center, axis=-1, keepdims=True)
    return center * lax.rsqrt(spread + norm_epsilon) * gain + shift


def exact_gelu(inner):
    return jax.nn.gelu(inner, approximate=False)


def block_scores(query_block, key_seq, segment_row, valid_count, first_row):
    block_rows = query_block.shape[0]
    length = key_seq.shape[0]
    scores = (
        jnp.einsum("qhd,khd->hqk", query_block, key_seq, preferred_element_type=jnp.float32) * 0.125
    )
    positions = jnp.arange(length, dtype=jnp.int32)
    query_pos = first_row + jnp.arange(block_rows, dtype=jnp.int32)
    query_seg = lax.dynamic_slice_in_dim(segment_row, first_row, block_rows)
    allowed = (query_seg[:, None] == segment_row[None, :]) & (
        (positions[None, :] < valid_count) | (query_pos[:, None] == positions[None, :])
    )
    return jnp.where(allowed[None], scores, masked_score)


def attend_sequence(pieces):
    query_seq, key_seq, value_seq, segment_row, valid_count = pieces
    length = query_seq.shape[0]
    block_rows = min(512, length)

    def one_block(block_index):
        first_row = block_index * block_rows
        query_block = lax.dynamic_slice_in_dim(query_seq, first_row, block_rows)
        masked = block_scores(query_block, key_seq, segment_row, valid_count, first_row)
        largest = jnp.max(masked, axis=-1, keepdims=True)
        totals = jnp.sum(jnp.exp(masked - largest), axis=-1, keepdims=True)
        log_total = largest + jnp.log(totals)
        probs_low = jnp.exp(masked - log_total).astype(jnp.bfloat16)
        context = jnp.einsum(
            "hqk,khd->qhd", probs_low, value_seq, preferred_element_type=jnp.float32
        )
        return (context.astype(jnp.bfloat16), log_total[..., 0])

    contexts, log_totals = lax.map(one_block, jnp.arange(length // block_rows, dtype=jnp.int32))
    return (contexts.reshape(query_seq.shape), log_totals)


def attend_backward(pieces):
    query_seq, key_seq, value_seq, segment_row, valid_count, grad_seq, log_totals = pieces
    length = query_seq.shape[0]
    block_rows = min(512, length)

    def one_block(running, inputs):
        key_grad, value_grad = running
        block_index, log_total = inputs
        first_row = block_index * block_rows
        query_block = lax.dynamic_slice_in_dim(query_seq, first_row, block_rows)
        grad_block = lax.dynamic_slice_in_dim(grad_seq, first_row, block_rows)
        masked = block_scores(query_block, key_seq, segment_row, valid_count, first_row)
        probs = jnp.exp(masked - log_total[..., None])
        probs_low = probs.astype(jnp.bfloat16)
        value_grad = value_grad + jnp.einsum(
            "hqk,qhd->khd", probs_low, grad_block, preferred_element_type=jnp.float32
        )
        d_probs = jnp.einsum(
            "qhd,khd->hqk", grad_block, value_seq, preferred_element_type=jnp.float32
        )
        row_inner = jnp.sum(probs * d_probs, axis=-1, keepdims=True)
        d_scores = (probs * (d_probs - row_inner)).astype(jnp.bfloat16)
        query_grad = (
            jnp.einsum("hqk,khd->qhd", d_scores, key_seq, preferred_element_type=jnp.float32)
            * 0.125
        )
        key_grad = (
            key_grad
            + jnp.einsum("hqk,qhd->khd", d_scores, query_block, preferred_element_type=jnp.float32)
            * 0.125
        )
        return ((key_grad, value_grad), query_grad.astype(jnp.bfloat16))

    empty = jnp.zeros(key_seq.shape, jnp.float32)
    block_ids = jnp.arange(length // block_rows, dtype=jnp.int32)
    (key_grad, value_grad), query_grads = lax.scan(
        one_block, (empty, empty), (block_ids, log_totals)
    )
    return (
        query_grads.reshape(query_seq.shape),
        key_grad.astype(jnp.bfloat16),
        value_grad.astype(jnp.bfloat16),
    )


def place_vector(local_part, whole, shard_index):
    width = local_part.shape[0]
    return lax.dynamic_update_slice_in_dim(
        jnp.zeros((whole,), jnp.float32), local_part, shard_index * width, 0
    )


def on_device(
    tokens,
    query_weight,
    query_bias,
    key_weight,
    value_weight,
    value_bias,
    output_weight,
    output_bias,
    first_gain,
    first_shift,
    inner_weight,
    inner_bias,
    outer_weight,
    outer_bias,
    second_gain,
    second_shift,
    segments,
    valid_length,
    cotangent,
):
    head_cols = query_weight.shape[1]
    hidden_cols = inner_weight.shape[1]
    local_heads = head_cols // HEAD_DIM
    shard_index = lax.axis_index("tensor")
    bias_query = lax.dynamic_slice_in_dim(query_bias, shard_index * head_cols, head_cols)
    bias_value = lax.dynamic_slice_in_dim(value_bias, shard_index * head_cols, head_cols)
    bias_inner = lax.dynamic_slice_in_dim(inner_bias, shard_index * hidden_cols, hidden_cols)
    full_query, full_key, full_value, full_output, full_inner, full_outer = (
        lax.all_gather(query_weight, "dp", axis=0, tiled=True),
        lax.all_gather(key_weight, "dp", axis=0, tiled=True),
        lax.all_gather(value_weight, "dp", axis=0, tiled=True),
        lax.all_gather(output_weight, "dp", axis=1, tiled=True),
        lax.all_gather(inner_weight, "dp", axis=0, tiled=True),
        lax.all_gather(outer_weight, "dp", axis=1, tiled=True),
    )
    group_rows = lax.all_gather(tokens, "tensor", axis=0, tiled=True)
    seq_count = segments.shape[0]
    seq_length = segments.shape[1]
    four_shape = (seq_count, seq_length, local_heads, HEAD_DIM)
    queries = (
        jnp.dot(group_rows, full_query, preferred_element_type=jnp.float32) + bias_query
    ).astype(jnp.bfloat16)
    keys_all = jnp.dot(group_rows, full_key, preferred_element_type=jnp.float32).astype(
        jnp.bfloat16
    )
    values_all = (
        jnp.dot(group_rows, full_value, preferred_element_type=jnp.float32) + bias_value
    ).astype(jnp.bfloat16)
    queries = queries.reshape(four_shape)
    keys_all = keys_all.reshape(four_shape)
    values_all = values_all.reshape(four_shape)
    contexts, log_totals = lax.map(
        attend_sequence, (queries, keys_all, values_all, segments, valid_length)
    )
    context = contexts.reshape(seq_count * seq_length, head_cols)
    partial_attn = jnp.dot(context, full_output, preferred_element_type=jnp.float32)
    attended = lax.psum_scatter(partial_attn, "tensor", scatter_dimension=0, tiled=True)
    first_sum = tokens.astype(jnp.float32) + attended + output_bias
    hidden = normalize(first_sum, first_gain, first_shift)
    ffn_rows = lax.all_gather(hidden.astype(jnp.bfloat16), "tensor", axis=0, tiled=True)
    inner = jnp.dot(ffn_rows, full_inner, preferred_element_type=jnp.float32) + bias_inner
    activated = exact_gelu(inner).astype(jnp.bfloat16)
    partial_ffn = jnp.dot(activated, full_outer, preferred_element_type=jnp.float32)
    outer = lax.psum_scatter(partial_ffn, "tensor", scatter_dimension=0, tiled=True)
    second_sum = hidden + outer + outer_bias
    final = normalize(second_sum, second_gain, second_shift)
    layer_output = final.astype(jnp.bfloat16)
    second_value, second_pull = jax.vjp(normalize, second_sum, second_gain, second_shift)
    d_second, second_gain_grad, second_shift_grad = second_pull(cotangent.astype(jnp.float32))
    outer_bias_grad = jnp.sum(d_second, axis=0)
    d_outer = d_second.astype(jnp.bfloat16)
    held = lax.optimization_barrier(
        (query_weight, key_weight, value_weight, output_weight, inner_weight, outer_weight, d_outer)
    )
    d_outer = held[6]
    back_query, back_key, back_value, back_output, back_inner, back_outer = (
        lax.all_gather(held[0], "dp", axis=0, tiled=True),
        lax.all_gather(held[1], "dp", axis=0, tiled=True),
        lax.all_gather(held[2], "dp", axis=0, tiled=True),
        lax.all_gather(held[3], "dp", axis=1, tiled=True),
        lax.all_gather(held[4], "dp", axis=0, tiled=True),
        lax.all_gather(held[5], "dp", axis=1, tiled=True),
    )
    outer_grad_rows = lax.all_gather(d_outer, "tensor", axis=0, tiled=True)
    outer_weight_grad = jnp.einsum(
        "gf,gd->fd", activated, outer_grad_rows, preferred_element_type=jnp.float32
    )
    d_activated = jnp.einsum(
        "gd,fd->gf", outer_grad_rows, back_outer, preferred_element_type=jnp.float32
    )
    gelu_value, gelu_pull = jax.vjp(exact_gelu, inner)
    d_inner = gelu_pull(d_activated)[0].astype(jnp.bfloat16)
    inner_weight_grad = jnp.einsum(
        "gd,gf->df", ffn_rows, d_inner, preferred_element_type=jnp.float32
    )
    inner_bias_local = jnp.sum(d_inner, axis=0, dtype=jnp.float32)
    partial_hidden = jnp.einsum(
        "gf,df->gd", d_inner, back_inner, preferred_element_type=jnp.float32
    )
    d_hidden = d_second + lax.psum_scatter(
        partial_hidden, "tensor", scatter_dimension=0, tiled=True
    )
    first_value, first_pull = jax.vjp(normalize, first_sum, first_gain, first_shift)
    d_first, first_gain_grad, first_shift_grad = first_pull(d_hidden)
    output_bias_grad = jnp.sum(d_first, axis=0)
    attn_grad_rows = lax.all_gather(d_first.astype(jnp.bfloat16), "tensor", axis=0, tiled=True)
    output_weight_grad = jnp.einsum(
        "gc,gd->cd", context, attn_grad_rows, preferred_element_type=jnp.float32
    )
    d_context = jnp.einsum(
        "gd,cd->gc", attn_grad_rows, back_output, preferred_element_type=jnp.float32
    ).astype(jnp.bfloat16)
    d_queries, d_keys, d_values = lax.map(
        attend_backward,
        (
            queries,
            keys_all,
            values_all,
            segments,
            valid_length,
            d_context.reshape(four_shape),
            log_totals,
        ),
    )
    d_queries = d_queries.reshape(seq_count * seq_length, head_cols)
    d_keys = d_keys.reshape(seq_count * seq_length, head_cols)
    d_values = d_values.reshape(seq_count * seq_length, head_cols)
    query_weight_grad = jnp.einsum(
        "gd,gc->dc", group_rows, d_queries, preferred_element_type=jnp.float32
    )
    key_weight_grad = jnp.einsum(
        "gd,gc->dc", group_rows, d_keys, preferred_element_type=jnp.float32
    )
    value_weight_grad = jnp.einsum(
        "gd,gc->dc", group_rows, d_values, preferred_element_type=jnp.float32
    )
    query_bias_local = jnp.sum(d_queries, axis=0, dtype=jnp.float32)
    value_bias_local = jnp.sum(d_values, axis=0, dtype=jnp.float32)
    partial_input = jnp.einsum(
        "gc,dc->gd", d_queries, back_query, preferred_element_type=jnp.float32
    )
    partial_input = partial_input + jnp.einsum(
        "gc,dc->gd", d_keys, back_key, preferred_element_type=jnp.float32
    )
    partial_input = partial_input + jnp.einsum(
        "gc,dc->gd", d_values, back_value, preferred_element_type=jnp.float32
    )
    input_gradient = d_first + lax.psum_scatter(
        partial_input.astype(jnp.bfloat16), "tensor", scatter_dimension=0, tiled=True
    ).astype(jnp.float32)
    query_shard, key_shard, value_shard, output_shard, inner_shard, outer_shard = (
        lax.psum_scatter(query_weight_grad, "dp", scatter_dimension=0, tiled=True),
        lax.psum_scatter(key_weight_grad, "dp", scatter_dimension=0, tiled=True),
        lax.psum_scatter(value_weight_grad, "dp", scatter_dimension=0, tiled=True),
        lax.psum_scatter(output_weight_grad, "dp", scatter_dimension=1, tiled=True),
        lax.psum_scatter(inner_weight_grad, "dp", scatter_dimension=0, tiled=True),
        lax.psum_scatter(outer_weight_grad, "dp", scatter_dimension=1, tiled=True),
    )
    model_width = query_bias.shape[0]
    hidden_width = inner_bias.shape[0]
    query_bias_full = place_vector(query_bias_local, model_width, shard_index)
    value_bias_full = place_vector(value_bias_local, model_width, shard_index)
    inner_bias_full = place_vector(inner_bias_local, hidden_width, shard_index)
    summed = lax.psum(
        (
            query_bias_full,
            value_bias_full,
            output_bias_grad,
            first_gain_grad,
            first_shift_grad,
            inner_bias_full,
            outer_bias_grad,
            second_gain_grad,
            second_shift_grad,
        ),
        ("dp", "tensor"),
    )
    return (
        layer_output,
        input_gradient,
        query_shard,
        summed[0],
        key_shard,
        value_shard,
        summed[1],
        output_shard,
        summed[2],
        summed[3],
        summed[4],
        inner_shard,
        summed[5],
        outer_shard,
        summed[6],
        summed[7],
        summed[8],
    )


def solution(mesh):
    placed = (
        P(("dp", "tensor"), None),
        P("dp", "tensor"),
        P(),
        P("dp", "tensor"),
        P("dp", "tensor"),
        P(),
        P("tensor", "dp"),
        P(),
        P(),
        P(),
        P("dp", "tensor"),
        P(),
        P("tensor", "dp"),
        P(),
        P(),
        P(),
        P("dp", None),
        P("dp"),
        P(("dp", "tensor"), None),
    )
    return jax.shard_map(
        on_device,
        mesh=mesh,
        in_specs=placed,
        out_specs=(
            P(("dp", "tensor"), None),
            P(("dp", "tensor"), None),
            P("dp", "tensor"),
            P(),
            P("dp", "tensor"),
            P("dp", "tensor"),
            P(),
            P("tensor", "dp"),
            P(),
            P(),
            P(),
            P("dp", "tensor"),
            P(),
            P("tensor", "dp"),
            P(),
            P(),
            P(),
        ),
        check_vma=False,
    )
```

profile of v0, /device:TPU:0, one launch (start us, length us, event | category | flops | bytes accessed | tf_op | source)
XLA Modules:
  0.0 1077.9 jit_solution(17472114728465103642)
XLA Ops:
  10.3 25.1 %all_gather.49 = bf16[768,384]{1,0:T(8,128)(2,1)S(1)} all-gather(bf16[48,384]{1,0:T(8,128)(2,1)} %param.24), channel_id=1, replica_groups=mesh['dp'=16,'tensor'=2] {'dp'}, dimensions={0}, use_global_device_ids=true | all-gather | bytes 626688 | tf_op jit(solution)/shard_map/all_gather | solution.py:141
  54.7 20.7 %all_gather.51 = bf16[768,384]{1,0:T(8,128)(2,1)S(1)} all-gather(bf16[48,384]{1,0:T(8,128)(2,1)} %param.27), channel_id=1, replica_groups=mesh['dp'=16,'tensor'=2] {'dp'}, dimensions={0}, use_global_device_ids=true | all-gather | bytes 626688 | tf_op jit(solution)/shard_map/all_gather | solution.py:143
  75.4 20.7 %all_gather.52 = bf16[384,768]{0,1:T(8,128)(2,1)} all-gather(bf16[384,48]{0,1:T(8,128)(2,1)} %param.29), channel_id=1, replica_groups=mesh['dp'=16,'tensor'=2] {'dp'}, dimensions={1}, use_global_device_ids=true | all-gather | bytes 626688 | tf_op jit(solution)/shard_map/all_gather | solution.py:144
  100.2 34.8 %while.47 = (s32[]{:T(128)}, bf16[2,512,6,64]{1,3,2,0:T(8,128)(2,1)S(1)}, f32[2,6,512]{2,1,0:T(8,128)S(1)}, s32[2]{0:T(128)S(1)}, s32[1024]{0:T(1024)S(1)}, /*in...) while((s32[]{:T(128)}, ...), condition=%wide.region_3.4_spmd, body=%wide.region_0.3_spmd.sunk | while | flops 842201600 | bytes 92672240 | solution.py:56
  140.5 41.1 %reduce-scatter.17.cloned.1.call-done = f32[512,768]{1,0:T(8,128)} async-done(((f32[1024,768]{1,0:T(8,128)}), f32[512,768]{1,0:T(8,128)}) %reduce-scatter.17.cloned.1.call-update) | async-done | bytes 1572880 | tf_op jit(solution)/shard_map/reduce_scatter | solution.py:169
  185.7 26.4 %all-gather.11.cloned.1.call-done = bf16[1024,768]{1,0:T(8,128)(2,1)} async-done(((bf16[512,768]{1,0:T(8,128)(2,1)}), bf16[1024,768]{1,0:T(8,128)(2,1)}) %all-gather.11.cloned.1.call-update) | async-done | bytes 1572880 | tf_op jit(solution)/shard_map/all_gather | solution.py:172
  232.0 24.9 %all-gather.15.cloned.1.call-done = bf16[1536,768]{0,1:T(8,128)(2,1)} async-done(((bf16[1536,48]{0,1:T(8,128)(2,1)}), bf16[1536,768]{0,1:T(8,128)(2,1)}) %all-gather.15.cloned.1.call-update) | async-done | bytes 2359312 | tf_op jit(solution)/shard_map/all_gather | solution.py:146
  263.9 41.9 %reduce-scatter.19.cloned.1.call-done = f32[512,768]{1,0:T(8,128)} async-done(((f32[1024,768]{1,0:T(8,128)}), f32[512,768]{1,0:T(8,128)}) %reduce-scatter.19.cloned.1.call-update) | async-done | bytes 1572880 | tf_op jit(solution)/shard_map/reduce_scatter | solution.py:176
  315.8 25.2 %all-gather.17.cloned.1.call-done = bf16[1024,768]{1,0:T(8,128)(2,1)} async-done(((bf16[512,768]{1,0:T(8,128)(2,1)}), bf16[1024,768]{1,0:T(8,128)(2,1)}) %all-gather.17.cloned.1.call-update) | async-done | bytes 1572880 | tf_op jit(solution)/shard_map/all_gather | solution.py:196
  341.0 45.0 %all-gather.19.cloned.1.call-done = bf16[1536,768]{0,1:T(8,128)(2,1)} async-done(((bf16[1536,48]{0,1:T(8,128)(2,1)}), bf16[1536,768]{0,1:T(8,128)(2,1)}) %all-gather.19.cloned.1.call-update) | async-done | bytes 2359312 | tf_op jit(solution)/shard_map/all_gather | solution.py:194
  398.4 30.9 %all-gather.21.cloned.1.call-done = bf16[768,1536]{1,0:T(8,128)(2,1)} async-done(((bf16[48,1536]{1,0:T(8,128)(2,1)}), bf16[768,1536]{1,0:T(8,128)(2,1)}) %all-gather.21.cloned.1.call-update) | async-done | bytes 2359312 | tf_op jit(solution)/shard_map/all_gather | solution.py:193
  436.2 41.9 %reduce-scatter.21.cloned.1.call-done = f32[512,768]{1,0:T(8,128)} async-done(((f32[1024,768]{1,0:T(8,128)}), f32[512,768]{1,0:T(8,128)}) %reduce-scatter.21.cloned.1.call-update) | async-done | bytes 1572880 | tf_op jit(solution)/shard_map/reduce_scatter | solution.py:212
  485.0 23.1 %all_gather.60 = bf16[384,768]{0,1:T(8,128)(2,1)S(1)} all-gather(bf16[384,48]{0,1:T(8,128)(2,1)S(1)} %copy-done.23), channel_id=1, replica_groups=mesh['dp'=16,'tensor'=2] {'dp'}, dimensions={1}, use_global_device_ids=true | all-gather | bytes 626688 | tf_op jit(solution)/shard_map/all_gather | solution.py:192
  508.1 20.4 %all_gather.61 = bf16[768,384]{1,0:T(8,128)(2,1)} all-gather(bf16[48,384]{1,0:T(8,128)(2,1)S(1)} %copy-done.24), channel_id=1, replica_groups=mesh['dp'=16,'tensor'=2] {'dp'}, dimensions={0}, use_global_device_ids=true | all-gather | bytes 626688 | tf_op jit(solution)/shard_map/all_gather | solution.py:189
  528.6 22.0 %all_gather.62 = bf16[768,384]{1,0:T(8,128)(2,1)} all-gather(bf16[48,384]{1,0:T(8,128)(2,1)S(1)} %copy-done.25), channel_id=1, replica_groups=mesh['dp'=16,'tensor'=2] {'dp'}, dimensions={0}, use_global_device_ids=true | all-gather | bytes 626688 | tf_op jit(solution)/shard_map/all_gather | solution.py:190
  550.5 20.4 %all_gather.63 = bf16[768,384]{1,0:T(8,128)(2,1)} all-gather(bf16[48,384]{1,0:T(8,128)(2,1)S(1)} %copy-done.26), channel_id=1, replica_groups=mesh['dp'=16,'tensor'=2] {'dp'}, dimensions={0}, use_global_device_ids=true | all-gather | bytes 626688 | tf_op jit(solution)/shard_map/all_gather | solution.py:191
  575.1 57.7 %while.48 = (s32[]{:T(128)}, f32[1024,6,64]{0,2,1:T(8,128)S(1)}, f32[1024,6,64]{0,2,1:T(8,128)}, bf16[2,512,6,64]{1,3,2,0:T(8,128)(2,1)}, s32[2]{0:T(128)S(1)}, ...) while((s32[]{:T(128)}, f32[1024,6,64]{0,2,1:T(8,128)S(1)}, ...), condition=%wide.region_17.18_spmd.clone, body=%wide.region_15.17_spmd.clone.sunk | while | flops 2064906752 | bytes 144941456 | solution.py:95
  673.5 39.8 %all-reduce = (f32[768]{0:T(1024)}, f32[768]{0:T(1024)}, f32[768]{0:T(1024)}, f32[768]{0:T(1024)}, f32[768]{0:T(1024)}, /*index=5*/f32[3072]{0:T(1024)}, f32[768]{0:T(1024)}, f32[768]{0:T(1024)}, f32[768]{0:T(1024)}) all-reduce(f32[768]{0:T(1024)S(1)} %dynamic_update_slice.32, ...), channel_id=1, replica_groups=mesh['dp'=16,'tensor'=2] {'dp','tensor'}, use_global_device_ids=true, to_apply=%region_21.22 | all-reduce | flops 9216 | bytes 73728 | tf_op jit(solution)/shard_map/psum | solution.py:276
  715.8 29.6 %reduce-scatter.29.cloned.1.call-done = f32[1536,48]{0,1:T(8,128)} async-done(((f32[1536,768]{0,1:T(8,128)}), f32[1536,48]{0,1:T(8,128)}) %reduce-scatter.29.cloned.1.call-update) | async-done | bytes 294928 | tf_op jit(solution)/shard_map/reduce_scatter | solution.py:269
  745.5 79.0 %reduce-scatter.27.cloned.1.call-done = f32[48,1536]{1,0:T(8,128)} async-done(((f32[768,1536]{1,0:T(8,128)}), f32[48,1536]{1,0:T(8,128)}) %reduce-scatter.27.cloned.1.call-update) | async-done | bytes 294928 | tf_op jit(solution)/shard_map/reduce_scatter | solution.py:268
  824.4 61.6 %reduce-scatter.25.cloned.1.call-done = f32[384,48]{0,1:T(8,128)} async-done(((f32[384,768]{0,1:T(8,128)}), f32[384,48]{0,1:T(8,128)}) %reduce-scatter.25.cloned.1.call-update) | async-done | bytes 73744 | tf_op jit(solution)/shard_map/reduce_scatter | solution.py:267
  886.1 61.4 %reduce-scatter.35.cloned.1.call-done = f32[48,384]{1,0:T(8,128)} async-done(((f32[768,384]{1,0:T(8,128)}), f32[48,384]{1,0:T(8,128)}) %reduce-scatter.35.cloned.1.call-update) | async-done | bytes 73744
  947.4 61.5 %reduce-scatter.31.cloned.1.call-done = f32[48,384]{1,0:T(8,128)} async-done(((f32[768,384]{1,0:T(8,128)}), f32[48,384]{1,0:T(8,128)}) %reduce-scatter.31.cloned.1.call-update) | async-done | bytes 73744
  1008.9 61.2 %reduce-scatter.33.cloned.1.call-done = f32[48,384]{1,0:T(8,128)} async-done(((f32[768,384]{1,0:T(8,128)}), f32[48,384]{1,0:T(8,128)}) %reduce-scatter.33.cloned.1.call-update) | async-done | bytes 73744
  (239 shorter events, 234.1 us)
Async XLA Ops:
  8.0 88.0 %all-gather.9.cloned.1.call-start = ((), (), s32[]{:S(2)}) async-start(), calls=%async_computation.10 | async-start | bytes 2359296 | tf_op jit(solution)/shard_map/all_gather | solution.py:148
  8.8 172.9 %reduce-scatter.17.cloned.1.call-start = ((), (), s32[]{:S(2)}) async-start(), calls=%async_computation.11 | async-start | bytes 4718592 | tf_op jit(solution)/shard_map/reduce_scatter | solution.py:169
  137.0 44.7 %copy-start.13 = (bf16[512,768]{1,0:T(8,128)(2,1)S(1)}, bf16[512,768]{1,0:T(8,128)(2,1)}, u32[]{:S(2)}) copy-start(bf16[512,768]{1,0:T(8,128)(2,1)} %param.23) | copy-start | bytes 2359300
  137.0 44.7 %copy-start.36 = (f32[768]{0:T(1024)S(1)}, f32[768]{0:T(1024)}, u32[]{:S(2)}) copy-start(f32[768]{0:T(1024)} %param.30) | copy-start | bytes 9220
  139.7 46.0 %all-gather.13.cloned.1.call-start = ((), (), s32[]{:S(2)}) async-start(), calls=%async_computation.13 | async-start | bytes 2506752 | tf_op jit(solution)/shard_map/all_gather | solution.py:145
  140.3 71.8 %all-gather.11.cloned.1.call-start = ((), (), s32[]{:S(2)}) async-start(), calls=%async_computation.12 | async-start | bytes 2359296 | tf_op jit(solution)/shard_map/all_gather | solution.py:172
  185.0 72.0 %all-gather.15.cloned.1.call-start = ((), (), s32[]{:S(2)}) async-start(), calls=%async_computation.14 | async-start | bytes 2506752 | tf_op jit(solution)/shard_map/all_gather | solution.py:146
  185.5 120.2 %reduce-scatter.19.cloned.1.call-start = ((), (), s32[]{:S(2)}) async-start(), calls=%async_computation.15 | async-start | bytes 4718592 | tf_op jit(solution)/shard_map/reduce_scatter | solution.py:176
  263.8 44.3 %copy-start.12 = (bf16[512,768]{1,0:T(8,128)(2,1)S(1)}, bf16[512,768]{1,0:T(8,128)(2,1)}, u32[]{:S(2)}) copy-start(bf16[512,768]{1,0:T(8,128)(2,1)} %param.41) | copy-start | bytes 2359300
  263.9 44.3 %copy-start.30 = (f32[768]{0:T(1024)S(1)}, f32[768]{0:T(1024)}, u32[]{:S(2)}) copy-start(f32[768]{0:T(1024)} %param.37) | copy-start | bytes 9220
  263.9 77.1 %all-gather.17.cloned.1.call-start = ((), (), s32[]{:S(2)}) async-start(), calls=%async_computation.16 | async-start | bytes 2359296 | tf_op jit(solution)/shard_map/all_gather | solution.py:196
  313.8 72.1 %all-gather.19.cloned.1.call-start = ((), (), s32[]{:S(2)}) async-start(), calls=%async_computation.17 | async-start | bytes 2506752 | tf_op jit(solution)/shard_map/all_gather | solution.py:194
  314.6 114.7 %all-gather.21.cloned.1.call-start = ((), (), s32[]{:S(2)}) async-start(), calls=%async_computation.18 | async-start | bytes 2506752 | tf_op jit(solution)/shard_map/all_gather | solution.py:193
  315.3 162.8 %reduce-scatter.21.cloned.1.call-start = ((), (), s32[]{:S(2)}) async-start(), calls=%async_computation.19 | async-start | bytes 4718592 | tf_op jit(solution)/shard_map/reduce_scatter | solution.py:212
  436.2 134.8 %all-gather.23.cloned.1.call-start = ((), (), s32[]{:S(2)}) async-start(), calls=%async_computation.20 | async-start | bytes 2359296 | tf_op jit(solution)/shard_map/all_gather | solution.py:218
  482.1 46.5 %copy-start.25 = (bf16[48,384]{1,0:T(8,128)(2,1)S(1)}, bf16[48,384]{1,0:T(8,128)(2,1)}, u32[]{:S(2)}) copy-start(bf16[48,384]{1,0:T(8,128)(2,1)} %param.26) | copy-start | bytes 110596
  482.1 68.4 %copy-start.26 = (bf16[48,384]{1,0:T(8,128)(2,1)S(1)}, bf16[48,384]{1,0:T(8,128)(2,1)}, u32[]{:S(2)}) copy-start(bf16[48,384]{1,0:T(8,128)(2,1)} %param.27) | copy-start | bytes 110596
  484.9 228.4 %reduce-scatter.23.cloned.1.call-start = ((), (), s32[]{:S(2)}) async-start(), calls=%async_computation.21 | async-start | bytes 2359296 | tf_op jit(solution)/shard_map/reduce_scatter | solution.py:260
  641.2 104.2 %reduce-scatter.29.cloned.1.call-start = ((), (), s32[]{:S(2)}) async-start(), calls=%async_computation.24 | async-start | bytes 5013504 | tf_op jit(solution)/shard_map/reduce_scatter | solution.py:269
  648.4 176.0 %reduce-scatter.27.cloned.1.call-start = ((), (), s32[]{:S(2)}) async-start(), calls=%async_computation.23 | async-start | bytes 5013504 | tf_op jit(solution)/shard_map/reduce_scatter | solution.py:268
  655.7 230.4 %reduce-scatter.25.cloned.1.call-start = ((), (), s32[]{:S(2)}) async-start(), calls=%async_computation.22 | async-start | bytes 1253376 | tf_op jit(solution)/shard_map/reduce_scatter | solution.py:267
  660.4 287.1 %reduce-scatter.35.cloned.1.call-start = ((), (), s32[]{:S(2)}) async-start(), calls=%async_computation.27 | async-start | bytes 1253376
  664.1 344.8 %reduce-scatter.31.cloned.1.call-start = ((), (), s32[]{:S(2)}) async-start(), calls=%async_computation.25 | async-start | bytes 1253376
  667.8 402.3 %reduce-scatter.33.cloned.1.call-start = ((), (), s32[]{:S(2)}) async-start(), calls=%async_computation.26 | async-start | bytes 1253376
  (39 other events, 351.9 us)
Sparse Core Ops, SparseCore 0:
  10.4 29.8 all-gather.8
  139.8 41.8 reduce-scatter.16
  264.0 41.7 reduce-scatter.18
  436.3 41.7 reduce-scatter.20
  485.0 27.1 all-gather.22
Sparse Core Ops, SparseCore 1:
  142.5 40.8 all-gather.12
  185.3 26.7 all-gather.10
  214.3 42.6 all-gather.14
  313.9 27.0 all-gather.16
  343.3 42.6 all-gather.18
  388.2 40.9 all-gather.20
  641.3 23.6 reduce-scatter.22
  669.3 76.1 reduce-scatter.28
  749.8 74.6 reduce-scatter.26
  828.7 57.3 reduce-scatter.24
  890.1 57.2 reduce-scatter.34
  951.6 57.2 reduce-scatter.30
  1013.0 57.1 reduce-scatter.32
where the time goes:
time: 1090 us; the launch traced here: 1080 us
  waiting for transfers between devices  635 us (58%)
  blocking collectives  212 us (19%)
  matrix products  147 us (13%)
  other arithmetic  42.9 us (4%)
  local copies, waits for them, and re-layouts  20.5 us (2%)
  between operations  16.7 us (2%)
    unnamed x21, waiting for transfers between devices  187 us
    reduce_scatter x1, waiting for transfers between devices, on_device(): lax.psum_scatter(inner_weight_grad, 'dp', scatter_dimension=0, tiled=True)  79 us
    reduce_scatter x1, waiting for transfers between devices, on_device(): lax.psum_scatter(output_weight_grad, 'dp', scatter_dimension=1, tiled=True)  61.6 us
    all_gather x1, waiting for transfers between devices, on_device(): lax.all_gather(held[5], 'dp', axis=1, tiled=True)  45 us
    reduce_scatter x1, waiting for transfers between devices, on_device(): lax.psum_scatter(partial_hidden, 'tensor', scatter_dimension=0, tiled=True)  41.9 us
    reduce_scatter x1, waiting for transfers between devices, on_device(): lax.psum_scatter(partial_ffn, 'tensor', scatter_dimension=0, tiled=True)  41.9 us
    reduce_scatter x1, waiting for transfers between devices, on_device(): lax.psum_scatter(partial_attn, 'tensor', scatter_dimension=0, tiled=True)  41.1 us
    psum x1, blocking collectives, on_device(): lax.psum((query_bias_full, value_bias_full, output_bias_grad, first_gain_...  39.8 us
  transfers between devices with their start and end apart: 18, of which 14 were waited for; matrix products, arithmetic and copies ran while one was open for 6% of the time, Pallas kernels for 0%

commit v1 on v0

v1 whole, which is shorter than its diff:
```python
import jax
import jax.numpy as jnp
from jax import lax
from jax.sharding import PartitionSpec as P

HEAD_DIM = 64


norm_epsilon = 1e-12
masked_score = -1e30


def normalize(matrix, gain, shift):
    center = matrix - jnp.mean(matrix, axis=-1, keepdims=True)
    spread = jnp.mean(center * center, axis=-1, keepdims=True)
    return center * lax.rsqrt(spread + norm_epsilon) * gain + shift


def block_scores(query_block, key_seq, segment_row, valid_count, first_row):
    block_rows = query_block.shape[0]
    length = key_seq.shape[0]
    scores = (
        jnp.einsum("qhd,khd->hqk", query_block, key_seq, preferred_element_type=jnp.float32) * 0.125
    )
    positions = jnp.arange(length, dtype=jnp.int32)
    query_pos = first_row + jnp.arange(block_rows, dtype=jnp.int32)
    query_seg = lax.dynamic_slice_in_dim(segment_row, first_row, block_rows)
    allowed = (query_seg[:, None] == segment_row[None, :]) & (
        (positions[None, :] < valid_count) | (query_pos[:, None] == positions[None, :])
    )
    return jnp.where(allowed[None], scores, masked_score)


def attend_sequence(pieces):
    query_seq, key_seq, value_seq, segment_row, valid_count = pieces
    length = query_seq.shape[0]
    block_rows = min(512, length)

    def one_block(block_index):
        first_row = block_index * block_rows
        query_block = lax.dynamic_slice_in_dim(query_seq, first_row, block_rows)
        masked = block_scores(query_block, key_seq, segment_row, valid_count, first_row)
        largest = jnp.max(masked, axis=-1, keepdims=True)
        totals = jnp.sum(jnp.exp(masked - largest), axis=-1, keepdims=True)
        log_total = largest + jnp.log(totals)
        probs_low = jnp.exp(masked - log_total).astype(jnp.bfloat16)
        context = jnp.einsum(
            "hqk,khd->qhd", probs_low, value_seq, preferred_element_type=jnp.float32
        )
        return (context.astype(jnp.bfloat16), log_total[..., 0])

    contexts, log_totals = lax.map(one_block, jnp.arange(length // block_rows, dtype=jnp.int32))
    return (contexts.reshape(query_seq.shape), log_totals)


def attend_backward(pieces):
    query_seq, key_seq, value_seq, segment_row, valid_count, grad_seq, log_totals = pieces
    length = query_seq.shape[0]
    block_rows = min(512, length)

    def one_block(running, inputs):
        key_grad, value_grad = running
        block_index, log_total = inputs
        first_row = block_index * block_rows
        query_block = lax.dynamic_slice_in_dim(query_seq, first_row, block_rows)
        grad_block = lax.dynamic_slice_in_dim(grad_seq, first_row, block_rows)
        masked = block_scores(query_block, key_seq, segment_row, valid_count, first_row)
        probs = jnp.exp(masked - log_total[..., None])
        probs_low = probs.astype(jnp.bfloat16)
        value_grad = value_grad + jnp.einsum(
            "hqk,qhd->khd", probs_low, grad_block, preferred_element_type=jnp.float32
        )
        d_probs = jnp.einsum(
            "qhd,khd->hqk", grad_block, value_seq, preferred_element_type=jnp.float32
        )
        row_inner = jnp.sum(probs * d_probs, axis=-1, keepdims=True)
        d_scores = (probs * (d_probs - row_inner)).astype(jnp.bfloat16)
        query_grad = (
            jnp.einsum("hqk,khd->qhd", d_scores, key_seq, preferred_element_type=jnp.float32)
            * 0.125
        )
        key_grad = (
            key_grad
            + jnp.einsum("hqk,qhd->khd", d_scores, query_block, preferred_element_type=jnp.float32)
            * 0.125
        )
        return ((key_grad, value_grad), query_grad.astype(jnp.bfloat16))

    empty = jnp.zeros(key_seq.shape, jnp.float32)
    block_ids = jnp.arange(length // block_rows, dtype=jnp.int32)
    (key_grad, value_grad), query_grads = lax.scan(
        one_block, (empty, empty), (block_ids, log_totals)
    )
    return (
        query_grads.reshape(query_seq.shape),
        key_grad.astype(jnp.bfloat16),
        value_grad.astype(jnp.bfloat16),
    )


def slope_and_gelu(inner):
    rise = 0.5 * (1.0 + lax.erf(inner * 0.7071067811865476))
    density = jnp.exp(-0.5 * inner * inner) * 0.3989422804014327
    return inner * rise, rise + inner * density


def norm_backward(matrix, gain, grad):
    center = matrix - jnp.mean(matrix, axis=-1, keepdims=True)
    spread = jnp.mean(center * center, axis=-1, keepdims=True)
    scale = lax.rsqrt(spread + norm_epsilon)
    normed = center * scale
    d_normed = grad * gain
    pulled = scale * (
        d_normed
        - jnp.mean(d_normed, axis=-1, keepdims=True)
        - normed * jnp.mean(d_normed * normed, axis=-1, keepdims=True)
    )
    return pulled, jnp.sum(grad * normed, axis=0), jnp.sum(grad, axis=0)


def halves_in_order(mine, other, shard_index):
    first = shard_index == 0
    return jnp.where(first, mine, other), jnp.where(first, other, mine)


def mix(left, right, dims):
    return lax.dot_general(left, right, (dims, ((), ())), preferred_element_type=jnp.float32)


def on_device(
    tokens,
    query_weight,
    query_bias,
    key_weight,
    value_weight,
    value_bias,
    output_weight,
    output_bias,
    first_gain,
    first_shift,
    inner_weight,
    inner_bias,
    outer_weight,
    outer_bias,
    second_gain,
    second_shift,
    segments,
    valid_length,
    cotangent,
):
    low = jnp.bfloat16
    whole = ("tensor", "dp")
    swap = [(0, 1), (1, 0)]
    own_rows, width = tokens.shape
    head_cols = query_weight.shape[1]
    hidden_cols = inner_weight.shape[1]
    local_heads = head_cols // HEAD_DIM
    shard_index = lax.axis_index("tensor")
    own_start = shard_index * own_rows
    other_start = (1 - shard_index) * own_rows

    other_tokens = lax.ppermute(tokens, "tensor", swap)
    full_qkv = lax.all_gather(
        jnp.concatenate([query_weight, key_weight, value_weight], axis=1), "dp", axis=0, tiled=True
    )
    full_output = lax.all_gather(output_weight.T, whole, axis=0, tiled=True)
    full_inner = lax.all_gather(inner_weight, whole, axis=0, tiled=True)
    full_outer = lax.all_gather(outer_weight.T, whole, axis=0, tiled=True)
    full_output = full_output.reshape(2, width, head_cols)
    full_inner = full_inner.reshape(2, width, hidden_cols)
    full_outer = full_outer.reshape(2, width, hidden_cols)

    group_rows = jnp.concatenate(halves_in_order(tokens, other_tokens, shard_index), axis=0)
    bias_query = lax.dynamic_slice_in_dim(query_bias, shard_index * head_cols, head_cols)
    bias_value = lax.dynamic_slice_in_dim(value_bias, shard_index * head_cols, head_cols)
    bias_qkv = jnp.concatenate([bias_query, jnp.zeros_like(bias_query), bias_value])
    seq_count, seq_length = segments.shape
    four_shape = (seq_count, seq_length, local_heads, HEAD_DIM)
    qkv = (mix(group_rows, full_qkv, ((1,), (0,))) + bias_qkv).astype(low)
    queries = qkv[:, :head_cols].reshape(four_shape)
    keys_all = qkv[:, head_cols : 2 * head_cols].reshape(four_shape)
    values_all = qkv[:, 2 * head_cols :].reshape(four_shape)
    contexts, log_totals = lax.map(
        attend_sequence, (queries, keys_all, values_all, segments, valid_length)
    )
    context = contexts.reshape(seq_count * seq_length, head_cols)
    own_context = lax.dynamic_slice_in_dim(context, own_start, own_rows)
    far_context = lax.ppermute(
        lax.dynamic_slice_in_dim(context, other_start, own_rows), "tensor", swap
    )
    context_halves = halves_in_order(own_context, far_context, shard_index)
    attended = mix(context_halves[0], full_output[0], ((1,), (1,))) + mix(
        context_halves[1], full_output[1], ((1,), (1,))
    )
    first_sum = tokens.astype(jnp.float32) + attended + output_bias
    hidden = normalize(first_sum, first_gain, first_shift)
    hidden_low = hidden.astype(low)
    activated, slopes = [], []
    outer = outer_bias
    for half in range(2):
        inner = (
            mix(hidden_low, full_inner[half], ((1,), (0,)))
            + inner_bias[half * hidden_cols : (half + 1) * hidden_cols]
        )
        value, slope = slope_and_gelu(inner)
        activated.append(value.astype(low))
        slopes.append(slope)
        outer = outer + mix(activated[half], full_outer[half], ((1,), (1,)))
    second_sum = hidden + outer
    layer_output = normalize(second_sum, second_gain, second_shift).astype(low)
    d_second, second_gain_grad, second_shift_grad = norm_backward(
        second_sum, second_gain, cotangent.astype(jnp.float32)
    )
    outer_bias_grad = jnp.sum(d_second, axis=0)
    d_outer = d_second.astype(low)
    outer_weight_grad = jnp.stack(
        [mix(d_outer, activated[half], ((0,), (0,))).astype(low) for half in range(2)]
    )
    d_hidden = d_second
    inner_grads, inner_bias_parts = [], []
    for half in range(2):
        d_activated = mix(d_outer, full_outer[half], ((1,), (0,)))
        d_inner = (d_activated * slopes[half]).astype(low)
        inner_grads.append(mix(hidden_low, d_inner, ((0,), (0,))).astype(low))
        inner_bias_parts.append(jnp.sum(d_inner, axis=0, dtype=jnp.float32))
        d_hidden = d_hidden + mix(d_inner, full_inner[half], ((1,), (1,)))
    inner_weight_grad = jnp.stack(inner_grads)
    inner_bias_grad = jnp.concatenate(inner_bias_parts)
    d_first, first_gain_grad, first_shift_grad = norm_backward(first_sum, first_gain, d_hidden)
    output_bias_grad = jnp.sum(d_first, axis=0)
    d_attended = d_first.astype(low)
    output_weight_grad = jnp.stack(
        [mix(d_attended, context_halves[half], ((0,), (0,))).astype(low) for half in range(2)]
    )
    d_context_halves = [
        mix(d_attended, full_output[half], ((1,), (0,))).astype(low) for half in range(2)
    ]
    first = shard_index == 0
    own_d_context = jnp.where(first, d_context_halves[0], d_context_halves[1])
    far_d_context = lax.ppermute(
        jnp.where(first, d_context_halves[1], d_context_halves[0]), "tensor", swap
    )
    d_context = jnp.concatenate(
        halves_in_order(own_d_context, far_d_context, shard_index), axis=0
    )
    d_queries, d_keys, d_values = lax.map(
        attend_backward,
        (
            queries,
            keys_all,
            values_all,
            segments,
            valid_length,
            d_context.reshape(four_shape),
            log_totals,
        ),
    )
    flat = (seq_count * seq_length, head_cols)
    d_qkv = jnp.concatenate(
        [d_queries.reshape(flat), d_keys.reshape(flat), d_values.reshape(flat)], axis=1
    )
    qkv_weight_grad = mix(group_rows, d_qkv, ((0,), (0,))).astype(low)
    partial_input = mix(d_qkv, full_qkv, ((1,), (1,)))
    far_input = lax.ppermute(
        lax.dynamic_slice_in_dim(partial_input, other_start, own_rows).astype(low), "tensor", swap
    )
    input_gradient = (
        d_first
        + lax.dynamic_slice_in_dim(partial_input, own_start, own_rows)
        + far_input.astype(jnp.float32)
    )

    def scatter(partial, axes):
        return lax.psum_scatter(
            partial.reshape(-1, partial.shape[-1]), axes, scatter_dimension=0, tiled=True
        ).astype(jnp.float32)

    outer_shard = scatter(outer_weight_grad, whole).T
    inner_shard = scatter(inner_weight_grad, whole)
    output_shard = scatter(output_weight_grad, whole).T
    qkv_shard = scatter(qkv_weight_grad, ("dp",))
    bias_local = jnp.sum(d_qkv, axis=0, dtype=jnp.float32)
    spread_out = lax.dynamic_update_slice(
        jnp.zeros((2, width), jnp.float32),
        jnp.stack([bias_local[:head_cols], bias_local[2 * head_cols :]]),
        (0, shard_index * head_cols),
    )
    pieces = [
        spread_out.reshape(-1),
        output_bias_grad,
        first_gain_grad,
        first_shift_grad,
        outer_bias_grad,
        second_gain_grad,
        second_shift_grad,
        inner_bias_grad,
    ]
    summed = lax.psum(jnp.concatenate(pieces), ("dp", "tensor"))
    rows = summed[: 8 * width].reshape(8, width)
    return (
        layer_output,
        input_gradient,
        qkv_shard[:, :head_cols],
        rows[0],
        qkv_shard[:, head_cols : 2 * head_cols],
        qkv_shard[:, 2 * head_cols :],
        rows[1],
        output_shard,
        rows[2],
        rows[3],
        rows[4],
        inner_shard,
        summed[8 * width :],
        outer_shard,
        rows[5],
        rows[6],
        rows[7],
    )


def solution(mesh):
    placed = (
        P(("dp", "tensor"), None),
        P("dp", "tensor"),
        P(),
        P("dp", "tensor"),
        P("dp", "tensor"),
        P(),
        P("tensor", "dp"),
        P(),
        P(),
        P(),
        P("dp", "tensor"),
        P(),
        P("tensor", "dp"),
        P(),
        P(),
        P(),
        P("dp", None),
        P("dp"),
        P(("dp", "tensor"), None),
    )
    return jax.shard_map(
        on_device,
        mesh=mesh,
        in_specs=placed,
        out_specs=(
            P(("dp", "tensor"), None),
            P(("dp", "tensor"), None),
            P("dp", "tensor"),
            P(),
            P("dp", "tensor"),
            P("dp", "tensor"),
            P(),
            P("tensor", "dp"),
            P(),
            P(),
            P(),
            P("dp", "tensor"),
            P(),
            P("tensor", "dp"),
            P(),
            P(),
            P(),
        ),
        check_vma=False,
    )
```

time: 1090 us -> 665 us (0.61)
  waiting for transfers between devices: 635 us -> 386 us
  blocking collectives: 212 us -> 50.1 us
  matrix products: 147 us -> 122 us
    unnamed x21 -> x8, waiting for transfers between devices: 187 us -> 1.47 us
    all_gather x8 -> x0, blocking collectives: 172 us -> none  [the longest x1 25.1 us: on_device(): lax.all_gather(query_weight, 'dp', axis=0, tiled=True)]
    reduce_scatter x7 -> x4, waiting for transfers between devices: 295 us -> 214 us  [scatter(): lax.psum_scatter(partial.reshape(-1, partial.shape[-1]), axes, scatter_di...]
    dot_general x18 -> x21, matrix products: 84.8 us -> 51.2 us  [mix(): lax.dot_general(left, right, (dims, ((), ())), preferred_element_type=jnp...]
    ppermute x0 -> x4, waiting for transfers between devices: none -> 23.8 us  [the longest x1 16.1 us: on_device(): other_tokens = lax.ppermute(tokens, 'tensor', swap)]
    all_gather x8 -> x4, waiting for transfers between devices: 152 us -> 146 us  [the longest x1 60.2 us: on_device(): full_inner = lax.all_gather(inner_weight, whole, axis=0, tiled=True)]
  transfers between devices with their start and end apart: 18 -> 12, of which waited for: 14 -> 8; matrix products, arithmetic and copies ran while one was open for 6% -> 25% of each run, Pallas kernels for 0% -> 0%
where the time goes in v1:
time: 665 us; the launch traced here: 660 us
  waiting for transfers between devices  386 us (58%)
  matrix products  122 us (18%)
  blocking collectives  50.1 us (8%)
  other arithmetic  49.1 us (7%)
  local copies, waits for them, and re-layouts  25.9 us (4%)
  between operations  15.1 us (2%)
  starting transfers between devices  7.72 us (1%)
    reduce_scatter x4, waiting for transfers between devices, scatter(): lax.psum_scatter(partial.reshape(-1, partial.shape[-1]), axes, scatter_di...  214 us
    all_gather x1, waiting for transfers between devices, on_device(): full_inner = lax.all_gather(inner_weight, whole, axis=0, tiled=True)  60.2 us
    all_gather x1, waiting for transfers between devices, on_device(): full_outer = lax.all_gather(outer_weight.T, whole, axis=0, tiled=True)  55.4 us
    dot_general x21, matrix products, mix(): lax.dot_general(left, right, (dims, ((), ())), preferred_element_type=jnp...  51.2 us
    psum x1, blocking collectives, on_device(): summed = lax.psum(jnp.concatenate(pieces), ('dp', 'tensor'))  50.1 us
    all_gather x1, waiting for transfers between devices, on_device(): lax.all_gather(jnp.concatenate([query_weight, key_weight, value_weight],...  21.4 us
    ppermute x1, waiting for transfers between devices, on_device(): other_tokens = lax.ppermute(tokens, 'tensor', swap)  16.1 us
    dot_general x2, matrix products, one_block(): jnp.einsum('hqk,khd->qhd', probs_low, value_seq, preferred_element_type=j...  15.6 us
  transfers between devices with their start and end apart: 12, of which 8 were waited for; matrix products, arithmetic and copies ran while one was open for 25% of the time, Pallas kernels for 0%

profile of v1, /device:TPU:0, one launch (start us, length us, event | category | flops | bytes accessed | tf_op | source)
XLA Modules:
  0.0 659.9 jit_solution(15233943400228055662)
XLA Ops:
  14.9 16.1 %collective-permute-done = bf16[512,768]{1,0:T(8,128)(2,1)S(1)} collective-permute-done((bf16[512,768]{1,0:T(8,128)(2,1)}, bf16[512,768]{1,0:T(8,128)(2,1)S(1)}, u32[]{:S(2)}, u32[]{:S(2)}) %collective-permute-start) | collective-permute-done | bytes 786464 | tf_op jit(solution)/shard_map/ppermute | solution.py:162
  32.3 21.4 %all-gather.5.cloned.1.call-done = bf16[768,1152]{1,0:T(8,128)(2,1)} async-done(((bf16[48,1152]{1,0:T(8,128)(2,1)}), bf16[768,1152]{1,0:T(8,128)(2,1)}) %all-gather.5.cloned.1.call-update) | async-done | bytes 1769488 | tf_op jit(solution)/shard_map/all_gather | solution.py:163
  58.6 35.3 %while.47 = (s32[]{:T(128)}, bf16[2,512,6,64]{1,3,2,0:T(8,128)(2,1)S(1)}, f32[2,6,512]{2,1,0:T(8,128)S(1)}, s32[2]{0:T(128)S(1)}, s32[1024]{0:T(1024)S(1)}, /*in...) while((s32[]{:T(128)}, ...), condition=%wide.region_3.4_spmd, body=%wide.region_0.3_spmd.sunk | while | flops 842201600 | bytes 92672224 | solution.py:52
  68.7 7.8 %fusion.144 = bf16[2,512,6,64]{1,3,2,0:T(8,128)(2,1)S(1)} fusion(bf16[2,512,6,64]{1,3,2,0:T(8,128)(2,1)S(1)} %get-tuple-element.507, s32[]{:T(128)} %get-tuple-element.506, bf16[1024,6,64]{0,2,1:T(8,128)(2,1)S(1)} %get-tuple-element.527, f32[6,512,1024]{2,1,0:T(8,128)} %copy-done.2, f32[6,512]{1,0:T(8,128)S(1)} %get-tuple-element.477, ...), kind=kOutput, calls=%fused_computation.11.clone.1 | convolution fusion | flops 415432704 | bytes 14303236 | tf_op jit(solution)/shard_map/while/body/eval_jaxpr/while/body/eval_jaxpr/hqk,khd->qhd/dot_general | solution.py:47
  86.1 7.8 %fusion.144 = bf16[2,512,6,64]{1,3,2,0:T(8,128)(2,1)S(1)} fusion(bf16[2,512,6,64]{1,3,2,0:T(8,128)(2,1)S(1)} %get-tuple-element.507, s32[]{:T(128)} %get-tuple-element.506, bf16[1024,6,64]{0,2,1:T(8,128)(2,1)S(1)} %get-tuple-element.527, f32[6,512,1024]{2,1,0:T(8,128)} %copy-done.2, f32[6,512]{1,0:T(8,128)S(1)} %get-tuple-element.477, ...), kind=kOutput, calls=%fused_computation.11.clone.1 | convolution fusion | flops 415432704 | bytes 14303236 | tf_op jit(solution)/shard_map/while/body/eval_jaxpr/while/body/eval_jaxpr/hqk,khd->qhd/dot_general | solution.py:47
  100.4 9.1 %all-gather.7.cloned.1.call-done = bf16[1536,384]{1,0:T(8,128)(2,1)} async-done(((bf16[48,384]{1,0:T(8,128)(2,1)}), bf16[1536,384]{1,0:T(8,128)(2,1)}) %all-gather.7.cloned.1.call-update) | async-done | bytes 1179664 | tf_op jit(solution)/shard_map/all_gather | solution.py:166
  115.6 60.2 %all-gather.9.cloned.1.call-done = bf16[1536,1536]{1,0:T(8,128)(2,1)} async-done(((bf16[48,1536]{1,0:T(8,128)(2,1)}), bf16[1536,1536]{1,0:T(8,128)(2,1)}) %all-gather.9.cloned.1.call-update) | async-done | bytes 4718608 | tf_op jit(solution)/shard_map/all_gather | solution.py:167
  175.9 5.8 multiply_convert_fusion.1
  185.1 55.4 %all-gather.11.cloned.1.call-done = bf16[1536,1536]{1,0:T(8,128)(2,1)} async-done(((bf16[48,1536]{1,0:T(8,128)(2,1)}), bf16[1536,1536]{1,0:T(8,128)(2,1)}) %all-gather.11.cloned.1.call-update) | async-done | bytes 4718608 | tf_op jit(solution)/shard_map/all_gather | solution.py:168
  269.6 7.7 %collective-permute-done.2 = bf16[512,384]{1,0:T(8,128)(2,1)} collective-permute-done((bf16[512,384]{1,0:T(8,128)(2,1)}, bf16[512,384]{1,0:T(8,128)(2,1)}, u32[]{:S(2)}, u32[]{:S(2)}) %collective-permute-start.2) | collective-permute-done | bytes 393248 | tf_op jit(solution)/shard_map/ppermute | solution.py:240
  280.6 67.3 %while.48 = (s32[]{:T(128)}, f32[1024,6,64]{0,2,1:T(8,128)}, f32[1024,6,64]{0,2,1:T(8,128)}, bf16[2,512,6,64]{1,3,2,0:T(8,128)(2,1)}, s32[2]{0:T(128)S(1)}, /*in...) while((s32[]{:T(128)}, f32[1024,6,64]{0,2,1:T(8,128)}, ...), condition=%wide.region_14.15_spmd.clone, body=%wide.region_12.14_spmd.clone.sunk | while | flops 2064906752 | bytes 217293712 | solution.py:91
  285.5 6.3 multiply_reduce_fusion.7
  291.8 5.1 multiply_convert_fusion.4
  296.9 5.4 bitcast_add_fusion.4
  302.2 6.4 fusion.156
  308.6 4.9 bitcast_add_fusion.5
  318.1 6.3 multiply_reduce_fusion.7
  324.3 5.1 multiply_convert_fusion.4
  329.4 5.8 bitcast_add_fusion.4
  335.2 6.3 fusion.156
  341.5 6.0 bitcast_add_fusion.5
  378.4 50.1 %psum.7 = f32[9216]{0:T(1024)S(1)} all-reduce(f32[9216]{0:T(1024)S(1)} %constant_dynamic-update-slice_fusion), channel_id=1, replica_groups=mesh['dp'=16,'tensor'=2] {'dp','tensor'}, use_global_device_ids=true, to_apply=%region_25.26 | all-reduce | flops 9216 | bytes 73728 | tf_op jit(solution)/shard_map/psum | solution.py:298
  435.4 103.7 %reduce-scatter.11.cloned.1.call-done = bf16[48,1536]{1,0:T(8,128)(2,1)} async-done(((bf16[1536,1536]{1,0:T(8,128)(2,1)}), bf16[48,1536]{1,0:T(8,128)(2,1)}) %reduce-scatter.11.cloned.1.call-update) | async-done | bytes 147472 | tf_op jit(solution)/shard_map/reduce_scatter | solution.py:274
  540.7 110.5 %reduce-scatter.9.cloned.1.call-done = bf16[48,1536]{1,0:T(8,128)(2,1)} async-done(((bf16[1536,1536]{1,0:T(8,128)(2,1)}), bf16[48,1536]{1,0:T(8,128)(2,1)}) %reduce-scatter.9.cloned.1.call-update) | async-done | bytes 147472 | tf_op jit(solution)/shard_map/reduce_scatter | solution.py:274
  (266 shorter events, 127.9 us)
Async XLA Ops:
  7.2 46.5 %all-gather.5.cloned.1.call-start = ((), (), s32[]{:S(2)}) async-start(), calls=%async_computation.4 | async-start | bytes 1880064 | tf_op jit(solution)/shard_map/all_gather | solution.py:163
  8.7 100.8 %all-gather.7.cloned.1.call-start = ((), (), s32[]{:S(2)}) async-start(), calls=%async_computation.5 | async-start | bytes 1216512 | tf_op jit(solution)/shard_map/all_gather | solution.py:166
  9.5 166.4 %all-gather.9.cloned.1.call-start = ((), (), s32[]{:S(2)}) async-start(), calls=%async_computation.6 | async-start | bytes 4866048 | tf_op jit(solution)/shard_map/all_gather | solution.py:167
  10.2 230.4 %all-gather.11.cloned.1.call-start = ((), (), s32[]{:S(2)}) async-start(), calls=%async_computation.7 | async-start | bytes 4866048 | tf_op jit(solution)/shard_map/all_gather | solution.py:168
  10.3 20.8 %collective-permute-start = (bf16[512,768]{1,0:T(8,128)(2,1)}, bf16[512,768]{1,0:T(8,128)(2,1)S(1)}, u32[]{:S(2)}, u32[]{:S(2)}) collective-permute-start(bf16[512,768]{1,0:T(8,128)(2,1)} %param.23), channel_id=1, source_target_pairs={{0,1},{1,0},{2,3},{3,2},{4,5},{5,4},{6,7},{7,6},{8,9},{9,8},{10,11... | collective-permute-start | bytes 2359304 | tf_op jit(solution)/shard_map/ppermute | solution.py:162
  13.3 419.2 %reduce-scatter.7.cloned.1.call-start = ((), (), s32[]{:S(2)}) async-start(), calls=%async_computation.9 | async-start | bytes 1216512 | tf_op jit(solution)/shard_map/reduce_scatter | solution.py:274
  32.3 21.4 %copy-start.20 = (bf16[512,768]{1,0:T(8,128)(2,1)}, bf16[512,768]{1,0:T(8,128)(2,1)S(1)}, u32[]{:S(2)}) copy-start(bf16[512,768]{1,0:T(8,128)(2,1)S(1)} %get-tuple-element.315) | copy-start | bytes 2359300
  32.3 21.4 %copy-start.22 = (bf16[512,768]{1,0:T(8,128)(2,1)}, bf16[512,768]{1,0:T(8,128)(2,1)S(1)}, u32[]{:S(2)}) copy-start(bf16[512,768]{1,0:T(8,128)(2,1)S(1)} %get-tuple-element.316) | copy-start | bytes 2359300
  95.8 15.5 %copy-start.39 = (f32[768]{0:T(1024)S(1)}, f32[768]{0:T(1024)}, u32[]{:S(2)}) copy-start(f32[768]{0:T(1024)} %param.30) | copy-start | bytes 9220
  97.7 11.8 %collective-permute-start.1 = (bf16[512,384]{1,0:T(8,128)(2,1)}, bf16[512,384]{1,0:T(8,128)(2,1)S(1)}, u32[]{:S(2)}, u32[]{:S(2)}) collective-permute-start(bf16[512,384]{1,0:T(8,128)(2,1)} %copy.53), channel_id=1, source_target_pairs={{0,1},{1,0},{2,3},{3,2},{4,5},{5,4},{6,7},{7,6},{8,9},{9,8},{10,11... | collective-permute-start | bytes 1179656 | tf_op jit(solution)/shard_map/ppermute | solution.py:188
  265.7 11.6 %collective-permute-start.2 = (bf16[512,384]{1,0:T(8,128)(2,1)}, bf16[512,384]{1,0:T(8,128)(2,1)}, u32[]{:S(2)}, u32[]{:S(2)}) collective-permute-start(bf16[512,384]{1,0:T(8,128)(2,1)} %get-tuple-element.345), channel_id=1, source_target_pairs={{0,1},{1,0},{2,3},{3,2},{4,5},{5,4},{6,7},{7,6},{8,9},{9,8},{10,11... | collective-permute-start | bytes 1179656 | tf_op jit(solution)/shard_map/ppermute | solution.py:240
  268.4 8.9 %copy-start.25 = (bf16[512,384]{1,0:T(8,128)(2,1)S(1)}, bf16[512,384]{1,0:T(8,128)(2,1)}, u32[]{:S(2)}) copy-start(bf16[512,384]{1,0:T(8,128)(2,1)} %copy-done.24) | copy-start | bytes 1179652
  268.4 8.9 %copy-start.26 = (bf16[512,384]{1,0:T(8,128)(2,1)S(1)}, bf16[512,384]{1,0:T(8,128)(2,1)}, u32[]{:S(2)}) copy-start(bf16[512,384]{1,0:T(8,128)(2,1)} %get-tuple-element.346) | copy-start | bytes 1179652
  269.6 164.3 %reduce-scatter.5.cloned.1.call-start = ((), (), s32[]{:S(2)}) async-start(), calls=%async_computation.8 | async-start | bytes 1880064 | tf_op jit(solution)/shard_map/reduce_scatter | solution.py:274
  296.9 11.7 %copy-start.1 = (f32[6,512,1024]{2,1,0:T(8,128)S(1)}, f32[6,512,1024]{2,1,0:T(8,128)}, u32[]{:S(2)}) copy-start(f32[6,512,1024]{2,1,0:T(8,128)} %copy-done) | copy-start | bytes 37748740 | tf_op jit(solution)/shard_map/while/body/eval_jaxpr/while
  329.4 12.1 %copy-start.1 = (f32[6,512,1024]{2,1,0:T(8,128)S(1)}, f32[6,512,1024]{2,1,0:T(8,128)}, u32[]{:S(2)}) copy-start(f32[6,512,1024]{2,1,0:T(8,128)} %copy-done) | copy-start | bytes 37748740 | tf_op jit(solution)/shard_map/while/body/eval_jaxpr/while
  355.5 183.6 %reduce-scatter.11.cloned.1.call-start = ((), (), s32[]{:S(2)}) async-start(), calls=%async_computation.11 | async-start | bytes 4866048 | tf_op jit(solution)/shard_map/reduce_scatter | solution.py:274
  362.5 288.8 %reduce-scatter.9.cloned.1.call-start = ((), (), s32[]{:S(2)}) async-start(), calls=%async_computation.10 | async-start | bytes 4866048 | tf_op jit(solution)/shard_map/reduce_scatter | solution.py:274
  371.1 7.1 %copy-start.30 = (f32[768]{0:T(1024)S(1)}, f32[768]{0:T(1024)}, u32[]{:S(2)}) copy-start(f32[768]{0:T(1024)} %get-tuple-element.253) | copy-start | bytes 9220
  371.1 7.1 %copy-start.29 = (f32[768]{0:T(1024)S(1)}, f32[768]{0:T(1024)}, u32[]{:S(2)}) copy-start(f32[768]{0:T(1024)} %get-tuple-element.258) | copy-start | bytes 9220
  371.2 7.2 %copy-start.34 = (f32[1536]{0:T(1024)S(1)}, f32[1536]{0:T(1024)}, u32[]{:S(2)}) copy-start(f32[1536]{0:T(1024)} %get-tuple-element.347) | copy-start | bytes 18436
  371.2 7.2 %copy-start.35 = (f32[1536]{0:T(1024)S(1)}, f32[1536]{0:T(1024)}, u32[]{:S(2)}) copy-start(f32[1536]{0:T(1024)} %get-tuple-element.349) | copy-start | bytes 18436
  376.6 53.0 %copy-start.9 = (f32[512,768]{1,0:T(8,128)S(1)}, f32[512,768]{1,0:T(8,128)}, u32[]{:S(2)}) copy-start(f32[512,768]{1,0:T(8,128)} %copy-done.8) | copy-start | bytes 4718596
  376.7 53.0 %collective-permute-start.3 = (bf16[512,768]{1,0:T(8,128)(2,1)S(1)}, bf16[512,768]{1,0:T(8,128)(2,1)S(1)}, u32[]{:S(2)}, u32[]{:S(2)}) collective-permute-start(bf16[512,768]{1,0:T(8,128)(2,1)S(1)} %dynamic-slice_convert_fusion), channel_id=1, source_target_pairs={{0,1},{1,0},{2,3},{3,2},{4,5},{5,4},{6,7},{7,6},{8,9},{9,8},{10,11... | collective-permute-start | bytes 2359304 | tf_op jit(solution)/shard_map/ppermute | solution.py:264
  (47 other events, 182.0 us)
Sparse Core Ops, SparseCore 0:
  10.7 42.8 all-gather.4
  56.6 52.9 all-gather.6
  112.4 63.4 all-gather.8
  178.6 61.8 all-gather.10
  269.7 95.3 reduce-scatter.6
  368.7 58.4 reduce-scatter.4
  432.7 106.2 reduce-scatter.10
  544.6 106.6 reduce-scatter.8
